TPU v7x, 128 devices: a whole 4x4x4 slice. The times are simulated.
128 devices in a mesh: dp: 16 (over z, y), tensor: 8 (over x, core).
Axes of the slice: x: 4, y: 4, z: 4, core: 2. Of those that a mesh axis runs over, the one named last changes fastest.
Arguments:
- dense: bfloat16 [3072, 2048], P('dp'), may hold values from -8 to 8
- bottom_weight: bfloat16 [2048, 16384], P(None, 'tensor'), may hold values from -0.125 to 0.125
- bottom_bias: float32 [16384], P('tensor'), may hold values from -3 to 3
- cross_blocks: bfloat16 [80, 512, 512], P('tensor', 'dp'), may hold values from -0.25 to 0.25
- cross_bias: float32 [16384], P('tensor'), may hold values from -3 to 3
- cotangent: bfloat16 [3072, 16384], P('dp', 'tensor'), may hold values from -6 to 6
- in_blocks: int32 [8, 10], replicated, may hold values from 0 to 31, as said below
- out_blocks: int32 [8, 10], replicated, may hold values from 0 to 31, as said below
- live_slots: int32 [8], replicated, may hold values from 2 to 10, as said below
Outputs:
- cross_out: bfloat16 [3072, 16384], P('dp', 'tensor')
- grad_bottom: float32 [2048, 16384], P('dp', 'tensor')
- grad_bias_bottom: float32 [16384], P('tensor')
- grad_blocks: float32 [80, 512, 512], P('tensor', 'dp')
- grad_bias: float32 [16384], P('tensor')
Inputs may be any that keep to these rules, and one draw needn't show every extreme that they name: `in_blocks`: among the live slots of one tensor device, at most 2 have input blocks held by any one tensor device (blocks s * 16384 / (512 * 8) onward for device s), and this most is reached in every draw. `out_blocks`: among the live slots of one tensor device, at most 2 have output blocks held by any one tensor device, and this most is reached in every draw. `live_slots`: some tensor device has all 10 slots live.
All inputs are finite; a program needn't handle non-finite values.
Results may differ from a plain program's by a relative error of at most 0.014.
Values may be sent and summed in bfloat16 or wider, within the bound.
A program may use at most 128 MiB of HBM per device.

v0:
```python
import jax
import jax.numpy as jnp
from jax import lax
from jax.sharding import PartitionSpec as P

BLK = 512
SLOTS = 10


def slot_ranks(owner, alive):
    order = jnp.arange(owner.shape[1])
    earlier = order[None, :] < order[:, None]
    same = (owner[:, :, None] == owner[:, None, :]) & alive[:, None, :] & earlier[None, :, :]
    return jnp.sum(same.astype(jnp.int32), axis=2)


def post_table(owner_mine, rank_mine, alive_mine, groups, capacity):
    slot_count = owner_mine.shape[0]
    match = (
        (owner_mine[None, None, :] == jnp.arange(groups)[:, None, None])
        & (rank_mine[None, None, :] == jnp.arange(capacity)[None, :, None])
        & alive_mine[None, None, :]
    )
    chosen = jnp.sum(match.astype(jnp.int32) * jnp.arange(slot_count)[None, None, :], axis=2)
    filled = jnp.any(match, axis=2)
    return (chosen, filled)


def pack_parts(parts, chosen, filled):
    picked = jnp.take(parts, chosen.reshape(-1), axis=1) * filled.reshape(-1)[None, :, None].astype(
        parts.dtype
    )
    return picked.reshape(parts.shape[0], chosen.shape[0], chosen.shape[1] * parts.shape[2])


def collect_parts(received, owner, local, rank, alive, target, capacity, per_device):
    row_count, groups, span_width = received.shape
    block_width = span_width // capacity
    match = ((owner == target) & alive)[:, :, None] & (
        rank[:, :, None] == jnp.arange(capacity)[None, None, :]
    )
    matches = match[:, :, :, None] & (
        local[:, :, None, None] == jnp.arange(per_device)[None, None, None, :]
    )
    onehot = (
        jnp.sum(matches.astype(jnp.int32), axis=1)
        .reshape(groups * capacity, per_device)
        .astype(jnp.bfloat16)
    )
    flattened = received.reshape(row_count, groups * capacity, block_width)
    summed = jnp.einsum("rib,il->rlb", flattened, onehot, preferred_element_type=jnp.float32)
    return summed.reshape(row_count, per_device * block_width)


def on_device(
    dense,
    bottom_weight,
    bottom_bias,
    cross_blocks,
    cross_bias,
    cotangent,
    in_blocks,
    out_blocks,
    live_slots,
):
    groups = lax.axis_size("tensor")
    mine = lax.axis_index("tensor")
    row_count = dense.shape[0]
    local_width = bottom_weight.shape[1]
    per_device = local_width // BLK
    capacity = -(-SLOTS // groups)
    preact = jnp.dot(dense, bottom_weight, preferred_element_type=jnp.float32) + bottom_bias
    start = jax.nn.silu(preact).astype(jnp.bfloat16)
    start_wide = start.astype(jnp.float32)
    cot_wide = cotangent.astype(jnp.float32)
    grad_mixed = cot_wide * start_wide
    grad_mixed_low = grad_mixed.astype(jnp.bfloat16)
    alive = jnp.arange(SLOTS)[None, :] < live_slots[:, None]
    alive_mine = alive[mine]
    switch = alive_mine.astype(jnp.bfloat16)[None, :, None]
    in_owner = in_blocks // per_device
    in_local = in_blocks % per_device
    out_owner = out_blocks // per_device
    out_local = out_blocks % per_device
    in_rank = slot_ranks(in_owner, alive)
    out_rank = slot_ranks(out_owner, alive)
    whole_start = lax.all_gather(start, "tensor", axis=1, tiled=True)
    fetched = jnp.take(whole_start.reshape(row_count, -1, BLK), in_blocks[mine], axis=1)
    taken = fetched
    product = jnp.einsum(
        "rki,kij->rkj",
        taken,
        lax.all_gather(cross_blocks, "dp", axis=1, tiled=True),
        preferred_element_type=jnp.float32,
    )
    parts = product.astype(jnp.bfloat16) * switch
    chosen_out, filled_out = post_table(
        out_owner[mine], out_rank[mine], alive_mine, groups, capacity
    )
    arrived_parts = lax.all_to_all(
        pack_parts(parts, chosen_out, filled_out), "tensor", split_axis=1, concat_axis=1, tiled=True
    )
    mixed = (
        collect_parts(
            arrived_parts, out_owner, out_local, out_rank, alive, mine, capacity, per_device
        )
        + cross_bias
    )
    cross_out = (start_wide * mixed + start_wide).astype(jnp.bfloat16)
    whole_grad = lax.all_gather(grad_mixed_low, "tensor", axis=1, tiled=True)
    upstream = jnp.take(whole_grad.reshape(row_count, -1, BLK), out_blocks[mine], axis=1)
    upstream = upstream * switch
    backward = jnp.einsum(
        "rkj,kij->rki",
        upstream,
        lax.all_gather(cross_blocks, "dp", axis=1, tiled=True),
        preferred_element_type=jnp.float32,
    )
    back_parts = backward.astype(jnp.bfloat16)
    chosen_in, filled_in = post_table(in_owner[mine], in_rank[mine], alive_mine, groups, capacity)
    arrived_back = lax.all_to_all(
        pack_parts(back_parts, chosen_in, filled_in),
        "tensor",
        split_axis=1,
        concat_axis=1,
        tiled=True,
    )
    grad_start = collect_parts(
        arrived_back, in_owner, in_local, in_rank, alive, mine, capacity, per_device
    )
    block_terms = jnp.einsum("rki,rkj->kij", fetched, upstream, preferred_element_type=jnp.float32)
    grad_blocks = lax.psum_scatter(
        block_terms.astype(jnp.bfloat16), "dp", scatter_dimension=1, tiled=True
    ).astype(jnp.float32)
    grad_start = grad_start + cot_wide * mixed + cot_wide
    sigma = jax.nn.sigmoid(preact)
    grad_pre = grad_start * sigma * (1.0 + preact * (1.0 - sigma))
    grad_pre_low = grad_pre.astype(jnp.bfloat16)
    taken = dense
    grad_bottom = lax.psum_scatter(
        lax.dot_general(
            taken, grad_pre_low, (((0,), (0,)), ((), ())), preferred_element_type=jnp.float32
        ).astype(jnp.bfloat16),
        "dp",
        scatter_dimension=0,
        tiled=True,
    ).astype(jnp.float32)
    bias_sums = lax.psum((jnp.sum(grad_pre, axis=0), jnp.sum(grad_mixed, axis=0)), "dp")
    return (cross_out, grad_bottom, bias_sums[0], grad_blocks, bias_sums[1])


def solution(mesh):
    return jax.shard_map(
        on_device,
        mesh=mesh,
        in_specs=(
            P("dp", None),
            P(None, "tensor"),
            P("tensor"),
            P("tensor", "dp", None),
            P("tensor"),
            P("dp", "tensor"),
            P(),
            P(),
            P(),
        ),
        out_specs=(
            P("dp", "tensor"),
            P("dp", "tensor"),
            P("tensor"),
            P("tensor", "dp", None),
            P("tensor"),
        ),
        check_vma=False,
    )
```

profile of v0, /device:TPU:0, one launch (start us, length us, event | category | flops | bytes accessed | tf_op | source)
XLA Modules:
  0.0 400.9 jit_solution(8510571627176802936)
XLA Ops:
  8.3 7.8 %fusion.9 = (f32[2048]{0:T(1024)}, bf16[192,2048]{1,0:T(8,128)(2,1)}, f32[192,2048]{1,0:T(8,128)}) fusion(bf16[192,2048]{1,0:T(8,128)(2,1)} %param.18, f32[2048]{0:T(1024)} %param.15, bf16[192,2048]{1,0:T(8,128)(2,1)S(1)} %copy-done, bf16[2048,2048]{1,0:T(8,128)(2,1)} %param.14), kind=kOutput, calls=%fused_computation.28 | convolution fusion | flops 1614542848 | bytes 12337152 | tf_op jit(solution)/shard_map/dot_general | solution.py:72
  21.2 38.5 %all-gather.4.cloned.1.call-done = bf16[192,16384]{1,0:T(8,128)(2,1)} async-done(((bf16[192,2048]{1,0:T(8,128)(2,1)}), bf16[192,16384]{1,0:T(8,128)(2,1)}) %all-gather.4.cloned.1.call-update) | async-done | bytes 6291472 | tf_op jit(solution)/shard_map/all_gather | solution.py:87
  59.6 6.2 %copy.90 = bf16[24,32,8,512]{3,2,0,1:T(8,128)(2,1)} copy(bf16[24,32,8,512]{3,2,1,0:T(8,128)(2,1)} %bitcast.71) | data formatting | bytes 12582912 | tf_op jit(solution)/shard_map/reshape | solution.py:88
  65.8 37.0 %all-gather.8.cloned.1.call-done = bf16[192,16384]{1,0:T(8,128)(2,1)} async-done(((bf16[192,2048]{1,0:T(8,128)(2,1)}), bf16[192,16384]{1,0:T(8,128)(2,1)}) %all-gather.8.cloned.1.call-update) | async-done | bytes 6291472 | tf_op jit(solution)/shard_map/all_gather | solution.py:110
  102.9 6.3 %copy.89 = bf16[24,32,8,512]{3,2,0,1:T(8,128)(2,1)} copy(bf16[24,32,8,512]{3,2,1,0:T(8,128)(2,1)} %bitcast.72) | data formatting | bytes 12582912 | tf_op jit(solution)/shard_map/reshape | solution.py:111
  109.2 4.9 %gather_fusion = bf16[10,192,512]{2,1,0:T(8,128)(2,1)} fusion(bf16[192,32,512]{2,0,1:T(8,128)(2,1)} %bitcast.69, s32[1024]{0:T(1024)S(1)} %pad_clamp_fusion.3), kind=kCustom, calls=%fused_computation.clone | custom fusion | bytes 3932200 | tf_op jit(solution)/shard_map/jit(_take)/gather | solution.py:88
  117.8 5.8 %convolution_convert_fusion = bf16[10,512,512]{2,1,0:T(8,128)(2,1)} fusion(bf16[10,192,512]{2,1,0:T(8,128)(2,1)} %gather_fusion, pred[10]{0:T(512)(128)(4,1)} %get-tuple-element.65, bf16[10,192,512]{2,1,0:T(8,128)(2,1)S(1)} %gather_fusion.2, pred[10]{0:T(512)(128)(4,1)S(1)} %get-tuple-element.44, bf16[10]{0:T(256)(128)(2,1)} %get-tuple-element.50), kind=kOutput, calls=%fused_computation.9 | convolution fusion | flops 1012203520 | bytes 9175080 | tf_op jit(solution)/shard_map/rki,rkj->kij/dot_general | solution.py:131
  138.9 22.7 %all-gather.6.cloned.1.call-done = bf16[10,512,512]{2,1,0:T(8,128)(2,1)} async-done(((bf16[10,32,512]{2,1,0:T(8,128)(2,1)}), bf16[10,512,512]{2,1,0:T(8,128)(2,1)}) %all-gather.6.cloned.1.call-update) | async-done | bytes 5242896 | tf_op jit(solution)/shard_map/all_gather | solution.py:93
  161.6 5.7 %multiply_bitcast_fusion = bf16[192,10,512]{2,0,1:T(8,128)(2,1)} fusion(bf16[10,512,512]{2,1,0:T(8,128)(2,1)} %all-gather.6.cloned.1.call-done, bf16[10]{0:T(256)(128)(2,1)} %get-tuple-element.50, bf16[10,192,512]{2,1,0:T(8,128)(2,1)} %gather_fusion, pred[10]{0:T(512)(128)(4,1)} %get-tuple-element.65), kind=kOutput, calls=%fused_computation.20 | convolution fusion | flops 1009582080 | bytes 9175070 | tf_op jit(solution)/shard_map/rki,kij->rkj/dot_general | solution.py:90
  177.1 5.7 %reshape.254 = bf16[192,8,1024]{2,1,0:T(8,128)(2,1)} reshape(bf16[192,16,512]{2,1,0:T(8,128)(2,1)} %copy.62) | data formatting | bytes 6291456 | tf_op jit(solution)/shard_map/reshape | solution.py:33
  182.8 5.4 %copy.63 = bf16[192,8,1024]{2,0,1:T(8,128)(2,1)} copy(bf16[192,8,1024]{2,1,0:T(8,128)(2,1)} %reshape.254) | data formatting | bytes 6291456 | tf_op jit(solution)/shard_map/reshape | solution.py:33
  188.1 4.6 %all-to-all-start = ((bf16[192,8,1024]{2,0,1:T(8,128)(2,1)}), bf16[192,8,1024]{2,0,1:T(8,128)(2,1)}, u32[]{:S(2)}, u32[]{:S(2)}) async-start(bf16[192,8,1024]{2,0,1:T(8,128)(2,1)} %copy.63), calls=%async_computation | async-start | bytes 6291456 | tf_op jit(solution)/shard_map/all_to_all | solution.py:100
  201.6 5.8 %convert_bitcast_fusion.1 = bf16[192,10,512]{2,0,1:T(8,128)(2,1)} fusion(bf16[10,512,512]{2,1,0:T(8,128)(2,1)} %all-gather.6.cloned.1.call-done, bf16[10,192,512]{2,1,0:T(8,128)(2,1)S(1)} %gather_fusion.2, pred[10]{0:T(512)(128)(4,1)} %copy-done.21, bf16[10]{0:T(256)(128)(2,1)} %get-tuple-element.50), kind=kOutput, calls=%fused_computation.19 | convolution fusion | flops 1009582080 | bytes 9175070 | tf_op jit(solution)/shard_map/rkj,kij->rki/dot_general | solution.py:113
  217.3 5.7 %reshape.259 = bf16[192,8,1024]{2,1,0:T(8,128)(2,1)} reshape(bf16[192,16,512]{2,1,0:T(8,128)(2,1)} %copy.72) | data formatting | bytes 6291456 | tf_op jit(solution)/shard_map/reshape | solution.py:33
  223.0 5.3 %copy.73 = bf16[192,8,1024]{2,0,1:T(8,128)(2,1)} copy(bf16[192,8,1024]{2,1,0:T(8,128)(2,1)} %reshape.259) | data formatting | bytes 6291456 | tf_op jit(solution)/shard_map/reshape | solution.py:33
  236.6 5.3 %copy.64 = bf16[192,8,1024]{2,1,0:T(8,128)(2,1)} copy(bf16[192,8,1024]{2,0,1:T(8,128)(2,1)} %all-to-all-done) | data formatting | bytes 6291456 | tf_op jit(solution)/shard_map/all_to_all | solution.py:100
  241.9 5.7 %reshape.255 = bf16[192,16,512]{2,1,0:T(8,128)(2,1)} reshape(bf16[192,8,1024]{2,1,0:T(8,128)(2,1)} %copy.64) | data formatting | bytes 6291456 | tf_op jit(solution)/shard_map/reshape | solution.py:50
  250.7 23.4 %all-to-all-done.1 = bf16[192,8,1024]{2,0,1:T(8,128)(2,1)} async-done(((bf16[192,8,1024]{2,0,1:T(8,128)(2,1)}), bf16[192,8,1024]{2,0,1:T(8,128)(2,1)}, u32[]{:S(2)}, u32[]{:S(2)}) %all-to-all-start.1) | async-done | bytes 3145760 | tf_op jit(solution)/shard_map/all_to_all | solution.py:121
  274.0 5.2 %copy.74 = bf16[192,8,1024]{2,1,0:T(8,128)(2,1)} copy(bf16[192,8,1024]{2,0,1:T(8,128)(2,1)} %all-to-all-done.1) | data formatting | bytes 6291456 | tf_op jit(solution)/shard_map/all_to_all | solution.py:121
  279.3 5.6 %reshape.260 = bf16[192,16,512]{2,1,0:T(8,128)(2,1)} reshape(bf16[192,8,1024]{2,1,0:T(8,128)(2,1)} %copy.74) | data formatting | bytes 6291456 | tf_op jit(solution)/shard_map/reshape | solution.py:50
  290.9 5.6 %convert_bitcast_fusion = bf16[2048,2048]{0,1:T(8,128)(2,1)} fusion(bf16[192,2048]{1,0:T(8,128)(2,1)S(1)} %copy-done, bf16[192,2048]{1,0:T(8,128)(2,1)S(1)} %get-tuple-element.43), kind=kOutput, calls=%fused_computation.4 | convolution fusion | flops 1614807040 | bytes 9961472 | tf_op jit(solution)/shard_map/dot_general | solution.py:141
  296.6 12.3 %copy.81 = bf16[2048,2048]{1,0:T(8,128)(2,1)} copy(bf16[2048,2048]{0,1:T(8,128)(2,1)} %convert_bitcast_fusion) | data formatting | bytes 16777216
  309.5 72.9 %all-reduce = (f32[2048]{0:T(1024)}, f32[2048]{0:T(1024)}) all-reduce(f32[2048]{0:T(1024)S(1)} %get-tuple-element.42, f32[2048]{0:T(1024)S(1)} %copy-done.10), channel_id=1, replica_groups=mesh['dp'=16,'tensor'=8] {'dp'}, use_global_device_ids=true, to_apply=%region_10.13 | all-reduce | flops 4096 | bytes 32768 | tf_op jit(solution)/shard_map/psum | solution.py:148
  384.3 7.5 %reduce-scatter.7.cloned.1.call-done = bf16[128,2048]{1,0:T(8,128)(2,1)} async-done(((bf16[2048,2048]{1,0:T(8,128)(2,1)}), bf16[128,2048]{1,0:T(8,128)(2,1)}) %reduce-scatter.7.cloned.1.call-update) | async-done | bytes 524304
  (121 shorter events, 75.9 us)
Async XLA Ops:
  7.2 9.0 %copy-start.2 = (bf16[192,2048]{1,0:T(8,128)(2,1)S(1)}, bf16[192,2048]{1,0:T(8,128)(2,1)}, u32[]{:S(2)}) copy-start(bf16[192,2048]{1,0:T(8,128)(2,1)} %param.18) | copy-start | bytes 2359300
  7.2 52.4 %all-gather.4.cloned.1.call-start = ((), (), s32[]{:S(2)}) async-start(), calls=%async_computation.4 | async-start | bytes 7077888 | tf_op jit(solution)/shard_map/all_gather | solution.py:87
  16.1 3.2 copy-start.6
  16.1 3.2 copy-start.8
  16.1 3.2 copy-start.20
  16.1 86.8 %all-gather.8.cloned.1.call-start = ((), (), s32[]{:S(2)}) async-start(), calls=%async_computation.6 | async-start | bytes 7077888 | tf_op jit(solution)/shard_map/all_gather | solution.py:110
  18.5 143.1 %all-gather.6.cloned.1.call-start = ((), (), s32[]{:S(2)}) async-start(), calls=%async_computation.5 | async-start | bytes 5570560 | tf_op jit(solution)/shard_map/all_gather | solution.py:93
  19.2 363.2 %reduce-scatter.5.cloned.1.call-start = ((), (), s32[]{:S(2)}) async-start(), calls=%async_computation.7 | async-start | bytes 5570560 | tf_op jit(solution)/shard_map/reduce_scatter | solution.py:132
  20.0 45.9 %copy-start.12 = (pred[8,10]{1,0:T(8,128)(4,1)}, pred[8,10]{1,0:T(8,128)(4,1)S(1)}, u32[]{:S(2)}) copy-start(pred[8,10]{1,0:T(8,128)(4,1)S(1)} %get-tuple-element.57) | copy-start | bytes 244
  20.0 103.6 %copy-start.4 = (s32[8,10]{1,0:T(8,128)}, s32[8,10]{1,0:T(8,128)S(1)}, u32[]{:S(2)}) copy-start(s32[8,10]{1,0:T(8,128)S(1)} %get-tuple-element.53) | copy-start | bytes 964
  20.0 104.3 %copy-start.5 = (s32[8,10]{1,0:T(8,128)}, s32[8,10]{1,0:T(8,128)S(1)}, u32[]{:S(2)}) copy-start(s32[8,10]{1,0:T(8,128)S(1)} %get-tuple-element.56) | copy-start | bytes 964
  21.1 96.6 %copy-start.21 = (pred[10]{0:T(512)(128)(4,1)}, pred[10]{0:T(512)(128)(4,1)S(1)}, u32[]{:S(2)}) copy-start(pred[10]{0:T(512)(128)(4,1)S(1)} %get-tuple-element.44) | copy-start | bytes 34
  127.1 2.0 copy-start.17
  127.1 2.0 copy-start.18
  127.2 1.9 copy-start.16
  188.1 43.1 %all-to-all-start = ((bf16[192,8,1024]{2,0,1:T(8,128)(2,1)}), bf16[192,8,1024]{2,0,1:T(8,128)(2,1)}, u32[]{:S(2)}, u32[]{:S(2)}) async-start(bf16[192,8,1024]{2,0,1:T(8,128)(2,1)} %copy.63), calls=%async_computation | async-start | bytes 6291456 | tf_op jit(solution)/shard_map/all_to_all | solution.py:100
  207.4 4.2 %copy-start.19 = (bf16[16]{0:T(256)(128)(2,1)S(1)}, bf16[16]{0:T(256)(128)(2,1)}, u32[]{:S(2)}) copy-start(bf16[16]{0:T(256)(128)(2,1)} %reshape.263) | copy-start | bytes 100
  207.4 4.2 %copy-start.22 = (pred[16]{0:T(512)(128)(4,1)S(1)}, pred[16]{0:T(512)(128)(4,1)}, u32[]{:S(2)}) copy-start(pred[16]{0:T(512)(128)(4,1)} %compare_and_fusion.2) | copy-start | bytes 52
  228.3 7.5 %copy-start.7 = (s32[8,10]{1,0:T(8,128)S(1)}, s32[8,10]{1,0:T(8,128)}, u32[]{:S(2)}) copy-start(s32[8,10]{1,0:T(8,128)} %param.20) | copy-start | bytes 964
  228.3 7.5 %copy-start.13 = (pred[8,10]{1,0:T(8,128)(4,1)S(1)}, pred[8,10]{1,0:T(8,128)(4,1)}, u32[]{:S(2)}) copy-start(pred[8,10]{1,0:T(8,128)(4,1)} %get-tuple-element.52) | copy-start | bytes 244
  228.3 7.6 %copy-start.14 = (pred[8,10]{1,0:T(8,128)(4,1)S(1)}, pred[8,10]{1,0:T(8,128)(4,1)}, u32[]{:S(2)}) copy-start(pred[8,10]{1,0:T(8,128)(4,1)} %get-tuple-element.55) | copy-start | bytes 244
  228.3 7.8 %copy-start.9 = (s32[8,10]{1,0:T(8,128)S(1)}, s32[8,10]{1,0:T(8,128)}, u32[]{:S(2)}) copy-start(s32[8,10]{1,0:T(8,128)} %param.19) | copy-start | bytes 964
  231.2 42.9 %all-to-all-start.1 = ((bf16[192,8,1024]{2,0,1:T(8,128)(2,1)}), bf16[192,8,1024]{2,0,1:T(8,128)(2,1)}, u32[]{:S(2)}, u32[]{:S(2)}) async-start(bf16[192,8,1024]{2,0,1:T(8,128)(2,1)} %copy.73), calls=%async_computation.1 | async-start | bytes 6291456 | tf_op jit(solution)/shard_map/all_to_all | solution.py:121
  235.6 156.2 %reduce-scatter.7.cloned.1.call-start = ((), (), s32[]{:S(2)}) async-start(), calls=%async_computation.8 | async-start | bytes 8912896
  (6 other events, 6.8 us)
Sparse Core Ops, SparseCore 0:
  16.3 43.3 all-gather.3
  61.9 40.9 all-gather.7
  105.0 56.5 all-gather.5
  164.9 78.7 reduce-scatter.4
  309.0 82.7 reduce-scatter.6
where the time goes:
time: 403 us; the launch traced here: 401 us
  waiting for transfers between devices  133 us (33%)
  local copies, waits for them, and re-layouts  113 us (28%)
  blocking collectives  72.9 us (18%)
  matrix products  35.7 us (9%)
  other arithmetic  23.6 us (6%)
  between operations  14.1 us (3%)
  starting transfers between devices  9.25 us (2%)
    psum x1, blocking collectives, on_device(): lax.psum((jnp.sum(grad_pre, axis=0), jnp.sum(grad_mixed, axis=0)), 'dp')  72.9 us
    all_gather x1, waiting for transfers between devices, on_device(): whole_start = lax.all_gather(start, 'tensor', axis=1, tiled=True)  38.5 us
    all_gather x1, waiting for transfers between devices, on_device(): whole_grad = lax.all_gather(grad_mixed_low, 'tensor', axis=1, tiled=True)  37 us
    all_to_all x1, waiting for transfers between devices, on_device(): lax.all_to_all(pack_parts(back_parts, chosen_in, filled_in), 'tensor', sp...  23.4 us
    all_gather x1, waiting for transfers between devices, on_device(): lax.all_gather(cross_blocks, 'dp', axis=1, tiled=True)  22.7 us
    reshape x4, local copies, waits for them, and re-layouts, pack_parts(): picked.reshape(parts.shape[0], chosen.shape[0], chosen.shape[1] * parts.s...  22.1 us
    unnamed x51, local copies, waits for them, and re-layouts  19.4 us
    reshape x2, local copies, waits for them, and re-layouts, collect_parts(): flattened = received.reshape(row_count, groups * capacity, block_width)  11.3 us
  transfers between devices with their start and end apart: 7, of which 6 were waited for; matrix products, arithmetic and copies ran while one was open for 39% of the time, Pallas kernels for 0%

commit v1 on v0

--- a/solution.py
+++ b/solution.py
@@ -97,8 +97,10 @@
     chosen_out, filled_out = post_table(
         out_owner[mine], out_rank[mine], alive_mine, groups, capacity
     )
-    arrived_parts = lax.all_to_all(
-        pack_parts(parts, chosen_out, filled_out), "tensor", split_axis=1, concat_axis=1, tiled=True
+    vals = pack_parts(parts, chosen_out, filled_out)
+    after = jnp.stack(jnp.split(vals, lax.axis_size("tensor"), axis=1))
+    arrived_parts = jnp.concatenate(
+        lax.all_to_all(after, axis_name="tensor", split_axis=0, concat_axis=0), axis=1
     )
     mixed = (
         collect_parts(

time: 403 us -> 423 us (1.050)
  waiting for transfers between devices: 133 us -> 150 us
  local copies, waits for them, and re-layouts: 113 us -> 120 us
  other arithmetic: 23.6 us -> 18.5 us
    all_to_all x1, waiting for transfers between devices: 2.85 us -> 23.1 us  [on_device(): lax.all_to_all(after, axis_name='tensor', split_axis=0, concat_axis=0)]
    split x0 -> x1, local copies, waits for them, and re-layouts: none -> 17.6 us  [on_device(): after = jnp.stack(jnp.split(vals, lax.axis_size('tensor'), axis=1))]
    all_gather x1, waiting for transfers between devices: 22.7 us -> 34.2 us  [on_device(): lax.all_gather(cross_blocks, 'dp', axis=1, tiled=True)]
    all_to_all x1, waiting for transfers between devices: 23.4 us -> 13.8 us  [on_device(): lax.all_to_all(pack_parts(back_parts, chosen_in, filled_in), 'tensor', sp...]
    another operation x0 -> x2, local copies, waits for them, and re-layouts: none -> 6.5 us  [the longest x1 5.63 us: collect_parts(): flattened = received.reshape(row_count, groups * capacity, block_width)]
    reshape x2 -> x1, local copies, waits for them, and re-layouts: 11.3 us -> 5.66 us  [collect_parts(): flattened = received.reshape(row_count, groups * capacity, block_width)]
    reshape x4 -> x3, local copies, waits for them, and re-layouts: 22.1 us -> 16.7 us  [pack_parts(): picked.reshape(parts.shape[0], chosen.shape[0], chosen.shape[1] * parts.s...]
    all_to_all x1 -> x0, local copies, waits for them, and re-layouts: 5.28 us -> none  [on_device(): lax.all_to_all(pack_parts(parts, chosen_out, filled_out), 'tensor', split...]
where the time goes in v1:
time: 423 us; the launch traced here: 421 us
  waiting for transfers between devices  150 us (35%)
  local copies, waits for them, and re-layouts  120 us (28%)
  blocking collectives  72.9 us (17%)
  matrix products  35.9 us (8%)
  other arithmetic  18.5 us (4%)
  between operations  14.1 us (3%)
  starting transfers between devices  9.33 us (2%)
    psum x1, blocking collectives, on_device(): lax.psum((jnp.sum(grad_pre, axis=0), jnp.sum(grad_mixed, axis=0)), 'dp')  72.9 us
    all_gather x1, waiting for transfers between devices, on_device(): whole_grad = lax.all_gather(grad_mixed_low, 'tensor', axis=1, tiled=True)  37.1 us
    all_gather x1, waiting for transfers between devices, on_device(): lax.all_gather(cross_blocks, 'dp', axis=1, tiled=True)  34.2 us
    all_gather x1, waiting for transfers between devices, on_device(): whole_start = lax.all_gather(start, 'tensor', axis=1, tiled=True)  33.8 us
    unnamed x44, local copies, waits for them, and re-layouts  23.9 us
    all_to_all x1, waiting for transfers between devices, on_device(): lax.all_to_all(after, axis_name='tensor', split_axis=0, concat_axis=0)  23.1 us
    split x1, local copies, waits for them, and re-layouts, on_device(): after = jnp.stack(jnp.split(vals, lax.axis_size('tensor'), axis=1))  17.6 us
    reshape x3, local copies, waits for them, and re-layouts, pack_parts(): picked.reshape(parts.shape[0], chosen.shape[0], chosen.shape[1] * parts.s...  16.7 us
  transfers between devices with their start and end apart: 7, of which 6 were waited for; matrix products, arithmetic and copies ran while one was open for 39% of the time, Pallas kernels for 0%

profile of v1, /device:TPU:0, one launch (start us, length us, event | category | flops | bytes accessed | tf_op | source)
XLA Modules:
  0.0 421.1 jit_solution(9515800992910145573)
XLA Ops:
  8.3 7.8 %fusion.9 = (f32[2048]{0:T(1024)}, bf16[192,2048]{1,0:T(8,128)(2,1)}, f32[192,2048]{1,0:T(8,128)}) fusion(bf16[192,2048]{1,0:T(8,128)(2,1)} %param.18, f32[2048]{0:T(1024)} %param.15, bf16[192,2048]{1,0:T(8,128)(2,1)S(1)} %copy-done, bf16[2048,2048]{1,0:T(8,128)(2,1)} %param.14), kind=kOutput, calls=%fused_computation.28 | convolution fusion | flops 1614542848 | bytes 12337152 | tf_op jit(solution)/shard_map/dot_general | solution.py:72
  25.8 33.8 %all-gather.4.cloned.1.call-done = bf16[192,16384]{1,0:T(8,128)(2,1)} async-done(((bf16[192,2048]{1,0:T(8,128)(2,1)}), bf16[192,16384]{1,0:T(8,128)(2,1)}) %all-gather.4.cloned.1.call-update) | async-done | bytes 6291472 | tf_op jit(solution)/shard_map/all_gather | solution.py:87
  59.6 6.2 %copy.188 = bf16[24,32,8,512]{3,2,0,1:T(8,128)(2,1)} copy(bf16[24,32,8,512]{3,2,1,0:T(8,128)(2,1)} %bitcast.92) | data formatting | bytes 12582912 | tf_op jit(solution)/shard_map/reshape | solution.py:88
  65.8 37.1 %all-gather.8.cloned.1.call-done = bf16[192,16384]{1,0:T(8,128)(2,1)} async-done(((bf16[192,2048]{1,0:T(8,128)(2,1)}), bf16[192,16384]{1,0:T(8,128)(2,1)}) %all-gather.8.cloned.1.call-update) | async-done | bytes 6291472 | tf_op jit(solution)/shard_map/all_gather | solution.py:112
  102.9 6.3 %copy.187 = bf16[24,32,8,512]{3,2,0,1:T(8,128)(2,1)} copy(bf16[24,32,8,512]{3,2,1,0:T(8,128)(2,1)} %bitcast.93) | data formatting | bytes 12582912 | tf_op jit(solution)/shard_map/reshape | solution.py:113
  109.2 4.9 %gather_fusion = bf16[10,192,512]{2,1,0:T(8,128)(2,1)} fusion(bf16[192,32,512]{2,0,1:T(8,128)(2,1)} %bitcast.90, s32[1024]{0:T(1024)S(1)} %pad_clamp_fusion.3), kind=kCustom, calls=%fused_computation.clone | custom fusion | bytes 3932200 | tf_op jit(solution)/shard_map/jit(_take)/gather | solution.py:88
  117.9 5.8 %convolution_convert_fusion = bf16[10,512,512]{2,1,0:T(8,128)(2,1)} fusion(bf16[10,192,512]{2,1,0:T(8,128)(2,1)} %gather_fusion, pred[10]{0:T(512)(128)(4,1)} %get-tuple-element.108, bf16[10,192,512]{2,1,0:T(8,128)(2,1)S(1)} %gather_fusion.2, pred[10]{0:T(512)(128)(4,1)} %get-tuple-element.79, bf16[10]{0:T(256)(128)(2,1)} %get-tuple-element.85), kind=kOutput, calls=%fused_computation.9 | convolution fusion | flops 1012203520 | bytes 9175080 | tf_op jit(solution)/shard_map/rki,rkj->kij/dot_general | solution.py:133
  127.4 34.2 %all-gather.6.cloned.1.call-done = bf16[10,512,512]{2,1,0:T(8,128)(2,1)} async-done(((bf16[10,32,512]{2,1,0:T(8,128)(2,1)}), bf16[10,512,512]{2,1,0:T(8,128)(2,1)}) %all-gather.6.cloned.1.call-update) | async-done | bytes 5242896 | tf_op jit(solution)/shard_map/all_gather | solution.py:93
  161.6 5.7 %multiply_bitcast_fusion = bf16[192,10,512]{2,0,1:T(8,128)(2,1)} fusion(bf16[10,512,512]{2,1,0:T(8,128)(2,1)} %all-gather.6.cloned.1.call-done, bf16[10]{0:T(256)(128)(2,1)} %get-tuple-element.85, bf16[10,192,512]{2,1,0:T(8,128)(2,1)} %gather_fusion, pred[10]{0:T(512)(128)(4,1)} %get-tuple-element.108), kind=kOutput, calls=%fused_computation.20 | convolution fusion | flops 1009582080 | bytes 9175070 | tf_op jit(solution)/shard_map/rki,kij->rkj/dot_general | solution.py:90
  177.0 5.7 %reshape.254 = bf16[192,8,1024]{2,1,0:T(8,128)(2,1)} reshape(bf16[192,16,512]{2,1,0:T(8,128)(2,1)} %copy.145) | data formatting | bytes 6291456 | tf_op jit(solution)/shard_map/reshape | solution.py:33
  182.7 5.8 %convert_bitcast_fusion.1 = bf16[192,10,512]{2,0,1:T(8,128)(2,1)} fusion(bf16[10,512,512]{2,1,0:T(8,128)(2,1)} %all-gather.6.cloned.1.call-done, bf16[10,192,512]{2,1,0:T(8,128)(2,1)S(1)} %gather_fusion.2, pred[10]{0:T(512)(128)(4,1)} %get-tuple-element.79, bf16[10]{0:T(256)(128)(2,1)} %get-tuple-element.85), kind=kOutput, calls=%fused_computation.19 | convolution fusion | flops 1009582080 | bytes 9175070 | tf_op jit(solution)/shard_map/rkj,kij->rki/dot_general | solution.py:115
  198.3 5.7 %reshape.259 = bf16[192,8,1024]{2,1,0:T(8,128)(2,1)} reshape(bf16[192,16,512]{2,1,0:T(8,128)(2,1)} %copy.154) | data formatting | bytes 6291456 | tf_op jit(solution)/shard_map/reshape | solution.py:33
  204.0 5.3 %copy.155 = bf16[192,8,1024]{2,0,1:T(8,128)(2,1)} copy(bf16[192,8,1024]{2,1,0:T(8,128)(2,1)} %reshape.259) | data formatting | bytes 6291456 | tf_op jit(solution)/shard_map/reshape | solution.py:33
  213.7 17.6 %fusion.29 = (bf16[192,1,1024]{2,1,0:T(2,128)(2,1)S(1)}, bf16[192,1,1024]{2,1,0:T(2,128)(2,1)S(1)}, bf16[192,1,1024]{2,1,0:T(2,128)(2,1)S(1)}, bf16[192,1,1024]{...) fusion(bf16[192,8,1024]{2,1,0:T(8,128)(2,1)} %reshape.254), kind=kLoop, calls=%fused_computation.106 | loop fusion | bytes 6291456 | tf_op jit(solution)/shard_map/split | solution.py:101
  238.4 13.8 %all-to-all-done.1 = bf16[192,8,1024]{2,0,1:T(8,128)(2,1)} async-done(((bf16[192,8,1024]{2,0,1:T(8,128)(2,1)}), bf16[192,8,1024]{2,0,1:T(8,128)(2,1)}, u32[]{:S(2)}, u32[]{:S(2)}) %all-to-all-start.1) | async-done | bytes 3145760 | tf_op jit(solution)/shard_map/all_to_all | solution.py:123
  257.8 5.3 %copy.156 = bf16[192,8,1024]{2,1,0:T(8,128)(2,1)} copy(bf16[192,8,1024]{2,0,1:T(8,128)(2,1)} %all-to-all-done.1) | data formatting | bytes 6291456 | tf_op jit(solution)/shard_map/all_to_all | solution.py:123
  263.2 5.7 %reshape.260 = bf16[192,16,512]{2,1,0:T(8,128)(2,1)} reshape(bf16[192,8,1024]{2,1,0:T(8,128)(2,1)} %copy.156) | data formatting | bytes 6291456 | tf_op jit(solution)/shard_map/reshape | solution.py:50
  271.9 23.1 %all-to-all-done = bf16[8,192,1,1024]{3,1,2,0:T(8,128)(2,1)} async-done(((bf16[8,192,1,1024]{3,1,2,0:T(8,128)(2,1)}), bf16[8,192,1,1024]{3,1,2,0:T(8,128)(2,1)}, u32[]{:S(2)}, u32[]{:S(2)}) %all-to-all-start) | async-done | bytes 3145760 | tf_op jit(solution)/shard_map/all_to_all | solution.py:103
  295.1 5.3 %copy.146 = bf16[192,8,1,1024]{3,1,0,2:T(8,128)(2,1)} copy(bf16[192,8,1,1024]{3,0,2,1:T(8,128)(2,1)} %bitcast.8) | data formatting | bytes 6291456 | tf_op jit(solution)/shard_map/reshape | solution.py:102
  300.3 5.6 %reshape_reshape.3 = bf16[192,16,512]{2,1,0:T(8,128)(2,1)} reshape(bf16[192,8,1,1024]{3,1,0,2:T(8,128)(2,1)} %copy.146) | data formatting | bytes 6291456 | tf_op jit(solution)/shard_map/reshape;reshape | solution.py:50
  311.1 5.6 %convert_bitcast_fusion = bf16[2048,2048]{0,1:T(8,128)(2,1)} fusion(bf16[192,2048]{1,0:T(8,128)(2,1)S(1)} %copy-done, bf16[192,2048]{1,0:T(8,128)(2,1)S(1)} %get-tuple-element.78), kind=kOutput, calls=%fused_computation.4 | convolution fusion | flops 1614807040 | bytes 9961472 | tf_op jit(solution)/shard_map/dot_general | solution.py:143
  316.8 12.3 %copy.163 = bf16[2048,2048]{1,0:T(8,128)(2,1)} copy(bf16[2048,2048]{0,1:T(8,128)(2,1)} %convert_bitcast_fusion) | data formatting | bytes 16777216
  329.7 72.9 %all-reduce = (f32[2048]{0:T(1024)}, f32[2048]{0:T(1024)}) all-reduce(f32[2048]{0:T(1024)S(1)} %get-tuple-element.77, f32[2048]{0:T(1024)S(1)} %copy-done.8), channel_id=1, replica_groups=mesh['dp'=16,'tensor'=8] {'dp'}, use_global_device_ids=true, to_apply=%region_10.13 | all-reduce | flops 4096 | bytes 32768 | tf_op jit(solution)/shard_map/psum | solution.py:150
  404.5 7.5 %reduce-scatter.7.cloned.1.call-done = bf16[128,2048]{1,0:T(8,128)(2,1)} async-done(((bf16[2048,2048]{1,0:T(8,128)(2,1)}), bf16[128,2048]{1,0:T(8,128)(2,1)}) %reduce-scatter.7.cloned.1.call-update) | async-done | bytes 524304
  (115 shorter events, 68.1 us)
Async XLA Ops:
  7.2 1.1 copy-start
  7.2 9.0 %copy-start.2 = (bf16[192,2048]{1,0:T(8,128)(2,1)S(1)}, bf16[192,2048]{1,0:T(8,128)(2,1)}, u32[]{:S(2)}) copy-start(bf16[192,2048]{1,0:T(8,128)(2,1)} %param.18) | copy-start | bytes 2359300
  7.2 52.4 %all-gather.4.cloned.1.call-start = ((), (), s32[]{:S(2)}) async-start(), calls=%async_computation.4 | async-start | bytes 7077888 | tf_op jit(solution)/shard_map/all_gather | solution.py:87
  16.1 3.2 copy-start.4
  16.1 3.2 copy-start.6
  16.1 3.2 copy-start.13
  16.1 86.8 %all-gather.8.cloned.1.call-start = ((), (), s32[]{:S(2)}) async-start(), calls=%async_computation.6 | async-start | bytes 7077888 | tf_op jit(solution)/shard_map/all_gather | solution.py:112
  18.5 143.1 %all-gather.6.cloned.1.call-start = ((), (), s32[]{:S(2)}) async-start(), calls=%async_computation.5 | async-start | bytes 5570560 | tf_op jit(solution)/shard_map/all_gather | solution.py:93
  19.2 383.4 %reduce-scatter.5.cloned.1.call-start = ((), (), s32[]{:S(2)}) async-start(), calls=%async_computation.7 | async-start | bytes 5570560 | tf_op jit(solution)/shard_map/reduce_scatter | solution.py:134
  23.2 42.6 %copy-start.14 = (s32[16]{0:T(128)}, s32[16]{0:T(128)S(1)}, u32[]{:S(2)}) copy-start(s32[16]{0:T(128)S(1)} %reshape.258) | copy-start | bytes 196
  188.5 4.1 copy-start.12
  188.5 4.1 copy-start.15
  209.3 42.9 %all-to-all-start.1 = ((bf16[192,8,1024]{2,0,1:T(8,128)(2,1)}), bf16[192,8,1024]{2,0,1:T(8,128)(2,1)}, u32[]{:S(2)}, u32[]{:S(2)}) async-start(bf16[192,8,1024]{2,0,1:T(8,128)(2,1)} %copy.155), calls=%async_computation.1 | async-start | bytes 6291456 | tf_op jit(solution)/shard_map/all_to_all | solution.py:123
  238.4 18.7 %copy-start.5 = (s32[8,10]{1,0:T(8,128)S(1)}, s32[8,10]{1,0:T(8,128)}, u32[]{:S(2)}) copy-start(s32[8,10]{1,0:T(8,128)} %param.20) | copy-start | bytes 964
  238.4 18.7 %copy-start.10 = (pred[8,10]{1,0:T(8,128)(4,1)S(1)}, pred[8,10]{1,0:T(8,128)(4,1)}, u32[]{:S(2)}) copy-start(pred[8,10]{1,0:T(8,128)(4,1)} %get-tuple-element.87) | copy-start | bytes 244
  238.4 18.7 %copy-start.11 = (pred[8,10]{1,0:T(8,128)(4,1)S(1)}, pred[8,10]{1,0:T(8,128)(4,1)}, u32[]{:S(2)}) copy-start(pred[8,10]{1,0:T(8,128)(4,1)} %get-tuple-element.98) | copy-start | bytes 244
  238.4 19.0 %copy-start.7 = (s32[8,10]{1,0:T(8,128)S(1)}, s32[8,10]{1,0:T(8,128)}, u32[]{:S(2)}) copy-start(s32[8,10]{1,0:T(8,128)} %param.19) | copy-start | bytes 964
  252.2 42.9 %all-to-all-start = ((bf16[8,192,1,1024]{3,1,2,0:T(8,128)(2,1)}), bf16[8,192,1,1024]{3,1,2,0:T(8,128)(2,1)}, u32[]{:S(2)}, u32[]{:S(2)}) async-start(bf16[8,192,1,1024]{3,1,2,0:T(8,128)(2,1)} %bitcast_dynamic-update-slice_fusion), calls=%async_computation | async-start | bytes 6291456 | tf_op jit(solution)/shard_map/all_to_all | solution.py:103
  256.6 155.4 %reduce-scatter.7.cloned.1.call-start = ((), (), s32[]{:S(2)}) async-start(), calls=%async_computation.8 | async-start | bytes 8912896
  306.0 3.3 copy-start.1
  306.0 3.3 copy-start.3
  306.0 3.3 copy-start.9
  329.0 0.7 copy-start.8
Sparse Core Ops, SparseCore 0:
  16.3 43.3 all-gather.3
  61.9 40.9 all-gather.7
  105.0 56.5 all-gather.5
  164.9 78.7 reduce-scatter.4
  329.2 82.8 reduce-scatter.6
